TPU v7x, 32 devices: a whole 2x2x4 slice. The times are simulated.
32 devices in a mesh: ctx: 8 (over y, x, core), head: 4 (over z).
Axes of the slice: x: 2, y: 2, z: 4, core: 2. Of those that a mesh axis runs over, the one named last changes fastest.
Arguments:
- q_nope: bfloat16 [512, 8192], P('ctx', 'head'), may hold values from -0.59765625 to 0.59765625
- q_rope: bfloat16 [512, 4096], P('ctx', 'head'), may hold values from -6 to 6
- w_uk: bfloat16 [64, 128, 512], P('head'), may hold values from -0.5 to 0.5
- w_uv: bfloat16 [64, 512, 128], P('head'), may hold values from -0.25 to 0.25
- w_o: bfloat16 [8192, 7168], P('head'), may hold values from -0.0625 to 0.0625
- latent_cache: bfloat16 [576, 8192], P(None, 'ctx'), may hold values from -36 to 36
- group_start: int32 [1], replicated, may hold values from 2048 to 7680
Outputs:
- attention_out: bfloat16 [512, 7168], P('ctx', 'head')
All inputs are finite; a program needn't handle non-finite values.
Results may differ from a plain program's by a relative error of at most 0.02.
Values may be sent and summed in bfloat16 or wider, within the bound.
A program may use at most 128 MiB of HBM per device.

v0:
```python
import math
import jax
import jax.numpy as jnp
from jax import lax
from jax.sharding import PartitionSpec as P

LATENT = 512
ROPE = 64
NOPE = 128
VDIM = 128
masked_score = -1e30


def score_scale():
    return (NOPE + ROPE) ** (-0.5) * (0.1 * math.log(32.0) + 1.0) ** 2


def absorb_queries(q_nope, q_rope, w_uk):
    local_heads = w_uk.shape[0]
    tokens_here = q_nope.shape[0]
    nope_part = q_nope.reshape(tokens_here, local_heads, NOPE)
    latent_query = jnp.einsum(
        "thn,hnl->thl", nope_part, w_uk, preferred_element_type=jnp.float32
    ).astype(jnp.bfloat16)
    rope_part = q_rope.reshape(tokens_here, local_heads, ROPE)
    return jnp.concatenate([latent_query, rope_part], axis=2)


def block_scores_of(query_rows, row_position, key_block, key_start):
    scores = jnp.dot(query_rows, key_block, preferred_element_type=jnp.float32) * score_scale()
    key_position = key_start + jnp.arange(key_block.shape[1], dtype=jnp.int32)
    visible = key_position[None, :] <= row_position[:, None]
    return (jnp.where(visible, scores, masked_score), visible)


def latent_product(weights, key_block):
    return lax.dot_general(
        weights.astype(jnp.bfloat16),
        key_block[:LATENT],
        (((1,), (1,)), ((), ())),
        preferred_element_type=jnp.float32,
    )


def online_update(running, query_rows, row_position, key_block, key_start):
    best_sofar, denominator, numerator = running
    scores, visible = block_scores_of(query_rows, row_position, key_block, key_start)
    new_best = jnp.maximum(best_sofar, jnp.max(scores, axis=1))
    decay_factor = jnp.exp(best_sofar - new_best)
    weights = jnp.where(visible, jnp.exp(scores - new_best[:, None]), 0.0)
    denominator = denominator * decay_factor + jnp.sum(weights, axis=1)
    numerator = numerator * decay_factor[:, None] + latent_product(weights, key_block)
    return (new_best, denominator, numerator)


def value_heads(latent_out, w_uv):
    leading = latent_out.astype(jnp.bfloat16)
    remainder = (latent_out - leading.astype(jnp.float32)).astype(jnp.bfloat16)
    first_term = jnp.einsum("thl,hlv->thv", leading, w_uv, preferred_element_type=jnp.float32)
    second_term = jnp.einsum("thl,hlv->thv", remainder, w_uv, preferred_element_type=jnp.float32)
    return first_term + second_term


def on_device(q_nope, q_rope, w_uk, w_uv, w_o, latent_cache, group_start):
    local_heads = w_uk.shape[0]
    tokens_here = q_nope.shape[0]
    queries = absorb_queries(q_nope, q_rope, w_uk)
    query_width = queries.shape[2]
    query_rows = queries.reshape(tokens_here * local_heads, query_width)
    first_token = group_start[0] + lax.axis_index("ctx") * tokens_here
    token_position = first_token + jnp.arange(tokens_here, dtype=jnp.int32)
    row_position = jnp.repeat(token_position, local_heads)
    last_position = first_token + tokens_here - 1
    row_total = query_rows.shape[0]
    initial = (
        jnp.full((row_total,), masked_score, jnp.float32),
        jnp.zeros((row_total,), jnp.float32),
        jnp.zeros((row_total, LATENT), jnp.float32),
    )
    cache_piece = lax.all_gather(latent_cache, "ctx", axis=1, tiled=True)
    span_keys = cache_piece.shape[1]
    step_keys = math.gcd(span_keys, 1024)

    def advance(position, current):
        key_block = lax.dynamic_slice_in_dim(cache_piece, position * step_keys, step_keys, 1)
        key_start = position * step_keys
        return lax.cond(
            key_start <= last_position,
            lambda held_state: online_update(
                held_state, query_rows, row_position, key_block, key_start
            ),
            lambda held_state: held_state,
            current,
        )

    best_all, denominator, numerator = lax.fori_loop(0, span_keys // step_keys, advance, initial)
    latent_out = (numerator / denominator[:, None]).reshape(tokens_here, local_heads, LATENT)
    head_values = value_heads(latent_out, w_uv)
    head_out = head_values.reshape(tokens_here, local_heads * VDIM).astype(jnp.bfloat16)
    mixed_columns = lax.psum_scatter(
        lax.dot_general(
            w_o, head_out, (((0,), (1,)), ((), ())), preferred_element_type=jnp.float32
        ).astype(jnp.bfloat16),
        "head",
        scatter_dimension=0,
        tiled=True,
    ).astype(jnp.float32)
    return mixed_columns.T.astype(jnp.bfloat16)


def solution(mesh):
    placed = (
        P("ctx", "head"),
        P("ctx", "head"),
        P("head", None, None),
        P("head", None, None),
        P("head", None),
        P(None, "ctx"),
        P(),
    )
    return jax.shard_map(
        on_device, mesh=mesh, in_specs=placed, out_specs=P("ctx", "head"), check_vma=False
    )
```

profile of v0, /device:TPU:0, one launch (start us, length us, event | category | flops | bytes accessed | tf_op | source)
XLA Modules:
  0.0 189.2 jit_solution(10341991162294786922)
XLA Ops:
  6.5 0.7 all-gather.2.cloned.1.call-update
  7.3 0.0 reduce-scatter.2.cloned.1.call-start
  8.0 1.1 concatenate.9
  9.1 1.4 fusion.20
  10.5 0.6 copy.12
  11.1 1.2 pad_maximum_fusion
  12.3 58.4 %all-gather.2.cloned.1.call-done = bf16[576,8192]{1,0:T(8,128)(2,1)} async-done(((bf16[576,1024]{1,0:T(8,128)(2,1)}), bf16[576,8192]{1,0:T(8,128)(2,1)}) %all-gather.2.cloned.1.call-update) | async-done | bytes 9437200 | tf_op jit(solution)/shard_map/all_gather | solution.py:80
  70.7 1.6 broadcast_in_dim.29
  72.3 57.2 %while.18 = (s32[]{:T(128)}, f32[1024]{0:T(1024)S(1)}, f32[1024]{0:T(1024)S(1)}, f32[1024,512]{1,0:T(8,128)}, s32[]{:T(128)}, /*index=5*/bf16[576,8192]{1,0:T(8,...) while((s32[]{:T(128)}, f32[1024]{0:T(1024)S(1)}, ...), condition=%wide.region_5.6_spmd.clone, body=%wide.region_0.5_spmd.clone.sunk | while | flops 2299530240 | bytes 37069400 | solution.py:96
  72.3 9.5 %conditional.3 = ((f32[1024]{0:T(1024)S(1)}, f32[1024]{0:T(1024)S(1)}, f32[1024,512]{1,0:T(8,128)})) conditional(s32[]{:T(128)} %convert_element_type.82, (f32[1024]{0:T(1024)S(1)}, f32[1024]{0:T(1024)S(1)}, f32[1024,512]{1,0:T(8,128)}) %tuple.50, (s32[]{:T(128)}, s32[64]{0:T(128)S(1)}, bf16[576,8192]{1,0:T(8,128)(2,1)}, ...), branch_computations={%region_1.0_spmd, %region_2.4_spmd} | conditional | flops 2299530240 | bytes 37069192 | solution.py:87
  72.3 0.1 broadcast_in_dim.35
  72.3 0.1 le.27
  72.4 3.4 %fusion.2 = (f32[1024]{0:T(1024)S(1)}, f32[1024,1024]{1,0:T(8,128)S(1)}) fusion(s32[1024]{0:T(1024)S(1)} %le.27, s32[1024]{0:T(1024)S(1)} %iota_add_fusion, bf16[1024,576]{1,0:T(8,128)(2,1)S(1)} %get-tuple-element.214, bf16[576,8192]{1,0:T(8,128)(2,1)} %get-tuple-element.213, s32[]{:T(128)S(6)} %select_n.18), kind=kOutput, calls=%fused_computation.3 | convolution fusion | flops 1212152832 | bytes 6565892 | tf_op jit(solution)/shard_map/while/body/eval_jaxpr/cond/branch_1_fun/dot_general | solution.py:30
  75.9 1.5 fusion.4
  77.5 0.0 copy-done.1
  77.5 3.0 %multiply_add_fusion = f32[1024,512]{1,0:T(8,128)S(1)} fusion(f32[1024,512]{1,0:T(8,128)S(1)} %copy-done.1, f32[1024,1024]{1,0:T(8,128)S(1)} %get-tuple-element.275, f32[1024]{0:T(1024)S(1)} %max.4, s32[1024]{0:T(1024)S(1)} %le.27, s32[1024]{0:T(1024)S(1)} %iota_add_fusion, bf16[576,8192]{1,0:T(8,128)(2,1)} %get-tuple-element.213, s32[]{:T(128)S(6)} %select_n.18, ...), kind=kOutput, calls=%fused_computation.6 | convolution fusion | flops 1081081856 | bytes 9453572 | tf_op jit(solution)/shard_map/while/body/eval_jaxpr/cond/branch_1_fun/dot_general | solution.py:37
  80.5 1.3 copy-done.2
  81.8 9.5 %conditional.3 = ((f32[1024]{0:T(1024)S(1)}, f32[1024]{0:T(1024)S(1)}, f32[1024,512]{1,0:T(8,128)})) conditional(s32[]{:T(128)} %convert_element_type.82, (f32[1024]{0:T(1024)S(1)}, f32[1024]{0:T(1024)S(1)}, f32[1024,512]{1,0:T(8,128)}) %tuple.50, (s32[]{:T(128)}, s32[64]{0:T(128)S(1)}, bf16[576,8192]{1,0:T(8,128)(2,1)}, ...), branch_computations={%region_1.0_spmd, %region_2.4_spmd} | conditional | flops 2299530240 | bytes 37069192 | solution.py:87
  81.8 0.1 broadcast_in_dim.35
  81.9 0.1 le.27
  82.0 3.4 %fusion.2 = (f32[1024]{0:T(1024)S(1)}, f32[1024,1024]{1,0:T(8,128)S(1)}) fusion(s32[1024]{0:T(1024)S(1)} %le.27, s32[1024]{0:T(1024)S(1)} %iota_add_fusion, bf16[1024,576]{1,0:T(8,128)(2,1)S(1)} %get-tuple-element.214, bf16[576,8192]{1,0:T(8,128)(2,1)} %get-tuple-element.213, s32[]{:T(128)S(6)} %select_n.18), kind=kOutput, calls=%fused_computation.3 | convolution fusion | flops 1212152832 | bytes 6565892 | tf_op jit(solution)/shard_map/while/body/eval_jaxpr/cond/branch_1_fun/dot_general | solution.py:30
  85.4 1.5 fusion.4
  87.0 0.0 copy-done.1
  87.0 3.0 %multiply_add_fusion = f32[1024,512]{1,0:T(8,128)S(1)} fusion(f32[1024,512]{1,0:T(8,128)S(1)} %copy-done.1, f32[1024,1024]{1,0:T(8,128)S(1)} %get-tuple-element.275, f32[1024]{0:T(1024)S(1)} %max.4, s32[1024]{0:T(1024)S(1)} %le.27, s32[1024]{0:T(1024)S(1)} %iota_add_fusion, bf16[576,8192]{1,0:T(8,128)(2,1)} %get-tuple-element.213, s32[]{:T(128)S(6)} %select_n.18, ...), kind=kOutput, calls=%fused_computation.6 | convolution fusion | flops 1081081856 | bytes 9453572 | tf_op jit(solution)/shard_map/while/body/eval_jaxpr/cond/branch_1_fun/dot_general | solution.py:37
  90.0 1.3 copy-done.2
  91.3 9.5 %conditional.3 = ((f32[1024]{0:T(1024)S(1)}, f32[1024]{0:T(1024)S(1)}, f32[1024,512]{1,0:T(8,128)})) conditional(s32[]{:T(128)} %convert_element_type.82, (f32[1024]{0:T(1024)S(1)}, f32[1024]{0:T(1024)S(1)}, f32[1024,512]{1,0:T(8,128)}) %tuple.50, (s32[]{:T(128)}, s32[64]{0:T(128)S(1)}, bf16[576,8192]{1,0:T(8,128)(2,1)}, ...), branch_computations={%region_1.0_spmd, %region_2.4_spmd} | conditional | flops 2299530240 | bytes 37069192 | solution.py:87
  91.4 0.1 broadcast_in_dim.35
  91.4 0.1 le.27
  91.5 3.4 %fusion.2 = (f32[1024]{0:T(1024)S(1)}, f32[1024,1024]{1,0:T(8,128)S(1)}) fusion(s32[1024]{0:T(1024)S(1)} %le.27, s32[1024]{0:T(1024)S(1)} %iota_add_fusion, bf16[1024,576]{1,0:T(8,128)(2,1)S(1)} %get-tuple-element.214, bf16[576,8192]{1,0:T(8,128)(2,1)} %get-tuple-element.213, s32[]{:T(128)S(6)} %select_n.18), kind=kOutput, calls=%fused_computation.3 | convolution fusion | flops 1212152832 | bytes 6565892 | tf_op jit(solution)/shard_map/while/body/eval_jaxpr/cond/branch_1_fun/dot_general | solution.py:30
  95.0 1.5 fusion.4
  96.5 0.0 copy-done.1
  96.6 3.0 %multiply_add_fusion = f32[1024,512]{1,0:T(8,128)S(1)} fusion(f32[1024,512]{1,0:T(8,128)S(1)} %copy-done.1, f32[1024,1024]{1,0:T(8,128)S(1)} %get-tuple-element.275, f32[1024]{0:T(1024)S(1)} %max.4, s32[1024]{0:T(1024)S(1)} %le.27, s32[1024]{0:T(1024)S(1)} %iota_add_fusion, bf16[576,8192]{1,0:T(8,128)(2,1)} %get-tuple-element.213, s32[]{:T(128)S(6)} %select_n.18, ...), kind=kOutput, calls=%fused_computation.6 | convolution fusion | flops 1081081856 | bytes 9453572 | tf_op jit(solution)/shard_map/while/body/eval_jaxpr/cond/branch_1_fun/dot_general | solution.py:37
  99.6 1.3 copy-done.2
  100.9 9.5 %conditional.3 = ((f32[1024]{0:T(1024)S(1)}, f32[1024]{0:T(1024)S(1)}, f32[1024,512]{1,0:T(8,128)})) conditional(s32[]{:T(128)} %convert_element_type.82, (f32[1024]{0:T(1024)S(1)}, f32[1024]{0:T(1024)S(1)}, f32[1024,512]{1,0:T(8,128)}) %tuple.50, (s32[]{:T(128)}, s32[64]{0:T(128)S(1)}, bf16[576,8192]{1,0:T(8,128)(2,1)}, ...), branch_computations={%region_1.0_spmd, %region_2.4_spmd} | conditional | flops 2299530240 | bytes 37069192 | solution.py:87
  100.9 0.1 broadcast_in_dim.35
  101.0 0.1 le.27
  101.0 3.4 %fusion.2 = (f32[1024]{0:T(1024)S(1)}, f32[1024,1024]{1,0:T(8,128)S(1)}) fusion(s32[1024]{0:T(1024)S(1)} %le.27, s32[1024]{0:T(1024)S(1)} %iota_add_fusion, bf16[1024,576]{1,0:T(8,128)(2,1)S(1)} %get-tuple-element.214, bf16[576,8192]{1,0:T(8,128)(2,1)} %get-tuple-element.213, s32[]{:T(128)S(6)} %select_n.18), kind=kOutput, calls=%fused_computation.3 | convolution fusion | flops 1212152832 | bytes 6565892 | tf_op jit(solution)/shard_map/while/body/eval_jaxpr/cond/branch_1_fun/dot_general | solution.py:30
  104.5 1.5 fusion.4
  106.1 0.0 copy-done.1
  106.1 3.0 %multiply_add_fusion = f32[1024,512]{1,0:T(8,128)S(1)} fusion(f32[1024,512]{1,0:T(8,128)S(1)} %copy-done.1, f32[1024,1024]{1,0:T(8,128)S(1)} %get-tuple-element.275, f32[1024]{0:T(1024)S(1)} %max.4, s32[1024]{0:T(1024)S(1)} %le.27, s32[1024]{0:T(1024)S(1)} %iota_add_fusion, bf16[576,8192]{1,0:T(8,128)(2,1)} %get-tuple-element.213, s32[]{:T(128)S(6)} %select_n.18, ...), kind=kOutput, calls=%fused_computation.6 | convolution fusion | flops 1081081856 | bytes 9453572 | tf_op jit(solution)/shard_map/while/body/eval_jaxpr/cond/branch_1_fun/dot_general | solution.py:37
  109.1 1.3 copy-done.2
  110.4 9.5 %conditional.3 = ((f32[1024]{0:T(1024)S(1)}, f32[1024]{0:T(1024)S(1)}, f32[1024,512]{1,0:T(8,128)})) conditional(s32[]{:T(128)} %convert_element_type.82, (f32[1024]{0:T(1024)S(1)}, f32[1024]{0:T(1024)S(1)}, f32[1024,512]{1,0:T(8,128)}) %tuple.50, (s32[]{:T(128)}, s32[64]{0:T(128)S(1)}, bf16[576,8192]{1,0:T(8,128)(2,1)}, ...), branch_computations={%region_1.0_spmd, %region_2.4_spmd} | conditional | flops 2299530240 | bytes 37069192 | solution.py:87
  110.4 0.1 broadcast_in_dim.35
  110.5 0.1 le.27
  110.6 3.4 %fusion.2 = (f32[1024]{0:T(1024)S(1)}, f32[1024,1024]{1,0:T(8,128)S(1)}) fusion(s32[1024]{0:T(1024)S(1)} %le.27, s32[1024]{0:T(1024)S(1)} %iota_add_fusion, bf16[1024,576]{1,0:T(8,128)(2,1)S(1)} %get-tuple-element.214, bf16[576,8192]{1,0:T(8,128)(2,1)} %get-tuple-element.213, s32[]{:T(128)S(6)} %select_n.18), kind=kOutput, calls=%fused_computation.3 | convolution fusion | flops 1212152832 | bytes 6565892 | tf_op jit(solution)/shard_map/while/body/eval_jaxpr/cond/branch_1_fun/dot_general | solution.py:30
  114.0 1.5 fusion.4
  115.6 0.0 copy-done.1
  115.6 3.0 %multiply_add_fusion = f32[1024,512]{1,0:T(8,128)S(1)} fusion(f32[1024,512]{1,0:T(8,128)S(1)} %copy-done.1, f32[1024,1024]{1,0:T(8,128)S(1)} %get-tuple-element.275, f32[1024]{0:T(1024)S(1)} %max.4, s32[1024]{0:T(1024)S(1)} %le.27, s32[1024]{0:T(1024)S(1)} %iota_add_fusion, bf16[576,8192]{1,0:T(8,128)(2,1)} %get-tuple-element.213, s32[]{:T(128)S(6)} %select_n.18, ...), kind=kOutput, calls=%fused_computation.6 | convolution fusion | flops 1081081856 | bytes 9453572 | tf_op jit(solution)/shard_map/while/body/eval_jaxpr/cond/branch_1_fun/dot_general | solution.py:37
  118.7 1.3 copy-done.2
  120.0 9.5 %conditional.3 = ((f32[1024]{0:T(1024)S(1)}, f32[1024]{0:T(1024)S(1)}, f32[1024,512]{1,0:T(8,128)})) conditional(s32[]{:T(128)} %convert_element_type.82, (f32[1024]{0:T(1024)S(1)}, f32[1024]{0:T(1024)S(1)}, f32[1024,512]{1,0:T(8,128)}) %tuple.50, (s32[]{:T(128)}, s32[64]{0:T(128)S(1)}, bf16[576,8192]{1,0:T(8,128)(2,1)}, ...), branch_computations={%region_1.0_spmd, %region_2.4_spmd} | conditional | flops 2299530240 | bytes 37069192 | solution.py:87
  120.0 0.1 broadcast_in_dim.35
  120.0 0.1 le.27
  120.1 3.4 %fusion.2 = (f32[1024]{0:T(1024)S(1)}, f32[1024,1024]{1,0:T(8,128)S(1)}) fusion(s32[1024]{0:T(1024)S(1)} %le.27, s32[1024]{0:T(1024)S(1)} %iota_add_fusion, bf16[1024,576]{1,0:T(8,128)(2,1)S(1)} %get-tuple-element.214, bf16[576,8192]{1,0:T(8,128)(2,1)} %get-tuple-element.213, s32[]{:T(128)S(6)} %select_n.18), kind=kOutput, calls=%fused_computation.3 | convolution fusion | flops 1212152832 | bytes 6565892 | tf_op jit(solution)/shard_map/while/body/eval_jaxpr/cond/branch_1_fun/dot_general | solution.py:30
  123.6 1.5 fusion.4
  125.2 0.0 copy-done.1
  125.2 3.0 %multiply_add_fusion = f32[1024,512]{1,0:T(8,128)S(1)} fusion(f32[1024,512]{1,0:T(8,128)S(1)} %copy-done.1, f32[1024,1024]{1,0:T(8,128)S(1)} %get-tuple-element.275, f32[1024]{0:T(1024)S(1)} %max.4, s32[1024]{0:T(1024)S(1)} %le.27, s32[1024]{0:T(1024)S(1)} %iota_add_fusion, bf16[576,8192]{1,0:T(8,128)(2,1)} %get-tuple-element.213, s32[]{:T(128)S(6)} %select_n.18, ...), kind=kOutput, calls=%fused_computation.6 | convolution fusion | flops 1081081856 | bytes 9453572 | tf_op jit(solution)/shard_map/while/body/eval_jaxpr/cond/branch_1_fun/dot_general | solution.py:37
  128.2 1.3 copy-done.2
  129.5 1.9 %broadcast_divide_fusion = f32[1024,512]{1,0:T(8,128)S(1)} fusion(f32[1024,512]{1,0:T(8,128)} %get-tuple-element.231, f32[1024]{0:T(1024)S(1)} %get-tuple-element.232), kind=kLoop, calls=%fused_computation.31 | loop fusion | flops 524288 | bytes 4198400 | tf_op jit(solution)/shard_map/div | solution.py:97
  131.5 0.3 copy-done.3
  131.7 1.3 fusion.19
  133.0 1.3 fusion.22
  134.4 13.1 %fusion.18 = bf16[7168,64]{0,1:T(8,128)(2,1)} fusion(bf16[2048,7168]{1,0:T(8,128)(2,1)} %param.15, bf16[16,8,8,128]{3,2,1,0:T(8,128)(2,1)S(1)} %fusion.22), kind=kOutput, calls=%fused_computation.21 | convolution fusion | flops 1879506944 | bytes 30539776 | tf_op jit(solution)/shard_map/dot_general | solution.py:101
  147.4 0.0 reduce-scatter.2.cloned.1.call-update
  147.5 34.9 %reduce-scatter.2.cloned.1.call-done = bf16[1792,64]{0,1:T(8,128)(2,1)} async-done(((bf16[7168,64]{0,1:T(8,128)(2,1)}), bf16[1792,64]{0,1:T(8,128)(2,1)}) %reduce-scatter.2.cloned.1.call-update) | async-done | bytes 229392 | tf_op jit(solution)/shard_map/reduce_scatter | solution.py:100
  (47 shorter events, 0.2 us)
Async XLA Ops:
  6.5 2.5 %copy-start = (bf16[16,128,512]{2,1,0:T(8,128)(2,1)S(1)}, bf16[16,128,512]{2,1,0:T(8,128)(2,1)}, u32[]{:S(2)}) copy-start(bf16[16,128,512]{2,1,0:T(8,128)(2,1)} %param.13) | copy-start | bytes 6291460
  6.5 64.2 %all-gather.2.cloned.1.call-start = ((), (), s32[]{:S(2)}) async-start(), calls=%async_computation.1 | async-start | bytes 10616832 | tf_op jit(solution)/shard_map/all_gather | solution.py:80
  7.3 175.1 %reduce-scatter.2.cloned.1.call-start = ((), (), s32[]{:S(2)}) async-start(), calls=%async_computation.2 | async-start | bytes 1146880 | tf_op jit(solution)/shard_map/reduce_scatter | solution.py:100
  12.3 60.0 %copy-start.4 = (bf16[1024,576]{1,0:T(8,128)(2,1)S(1)}, bf16[1024,576]{1,0:T(8,128)(2,1)}, u32[]{:S(2)}) copy-start(bf16[1024,576]{1,0:T(8,128)(2,1)} %pad_maximum_fusion) | copy-start | bytes 3538948
  75.9 1.6 copy-start.1
  80.5 1.3 copy-start.2
  85.4 1.6 copy-start.1
  90.0 1.3 copy-start.2
  95.0 1.6 copy-start.1
  99.6 1.3 copy-start.2
  104.5 1.6 copy-start.1
  109.1 1.3 copy-start.2
  114.0 1.6 copy-start.1
  118.6 1.3 copy-start.2
  123.6 1.6 copy-start.1
  128.2 1.3 copy-start.2
  129.5 2.2 %copy-start.3 = (bf16[16,512,128]{2,1,0:T(8,128)(2,1)S(1)}, bf16[16,512,128]{2,1,0:T(8,128)(2,1)}, u32[]{:S(2)}) copy-start(bf16[16,512,128]{2,1,0:T(8,128)(2,1)} %param.14) | copy-start | bytes 6291460
Sparse Core Ops, SparseCore 0:
  9.2 61.4 all-gather.1
  147.6 34.7 reduce-scatter.1
where the time goes:
time: 190 us; the launch traced here: 189 us
  waiting for transfers between devices  94 us (49%)
  matrix products  55.8 us (29%)
  between operations  14.1 us (7%)
  other arithmetic  12.5 us (7%)
  local copies, waits for them, and re-layouts  12.4 us (7%)
    all_gather x1, waiting for transfers between devices, on_device(): cache_piece = lax.all_gather(latent_cache, 'ctx', axis=1, tiled=True)  58.4 us
    reduce_scatter x1, waiting for transfers between devices, on_device(): lax.psum_scatter(lax.dot_general(w_o, head_out, (((0,), (1,)), ((), ())),...  34.9 us
    dot_general x6, matrix products, block_scores_of(): jnp.dot(query_rows, key_block, preferred_element_type=jnp.float32)  20.6 us
    dot_general x6, matrix products, latent_product(): lax.dot_general(weights.astype(jnp.bfloat16), key_block[:LATENT], (((1,),...  18.1 us
    dot_general x1, matrix products, on_device(): lax.dot_general(w_o, head_out, (((0,), (1,)), ((), ())), preferred_elemen...  13.1 us
    reduce_sum x6, other arithmetic, online_update(): denominator = denominator * decay_factor + jnp.sum(weights, axis=1)  9.27 us
    cond x30, local copies, waits for them, and re-layouts  7.95 us
  transfers between devices with their start and end apart: 2, of which 2 were waited for; matrix products, arithmetic and copies ran while one was open for 2% of the time, Pallas kernels for 0%

commit v1 on v0

--- a/solution.py
+++ b/solution.py
@@ -9,6 +9,24 @@
 NOPE = 128
 VDIM = 128
 masked_score = -1e30
+
+
+def laid_out(pieces, dim):
+    pieces = jnp.moveaxis(pieces, 0, dim)
+    shape = pieces.shape
+    return pieces.reshape(*shape[:dim], shape[dim] * shape[dim + 1], *shape[dim + 2 :])
+
+
+def doubled(array, axis):
+    length = lax.axis_size(axis)
+    blocks = array[None]
+    for level in range(length.bit_length() - 1):
+        distance = 1 << level
+        other = lax.ppermute(blocks, axis, [(i, i ^ distance) for i in range(length)])
+        both = jnp.stack([blocks, other])
+        upper = lax.axis_index(axis) >> level & 1
+        blocks = jnp.where(upper == 0, both, both[::-1]).reshape(-1, *array.shape)
+    return blocks
 
 
 def score_scale():
@@ -77,7 +95,7 @@
         jnp.zeros((row_total,), jnp.float32),
         jnp.zeros((row_total, LATENT), jnp.float32),
     )
-    cache_piece = lax.all_gather(latent_cache, "ctx", axis=1, tiled=True)
+    cache_piece = laid_out(doubled(latent_cache, "ctx"), 1)
     span_keys = cache_piece.shape[1]
     step_keys = math.gcd(span_keys, 1024)
 

time: 190 us -> 323 us (1.70)
  waiting for transfers between devices: 94 us -> 189 us
  other arithmetic: 12.5 us -> 46.1 us
  starting transfers between devices: 0.04 us -> 5.11 us
    ppermute x0 -> x3, waiting for transfers between devices: none -> 154 us  [doubled(): lax.ppermute(blocks, axis, [(i, i ^ distance) for i in range(length)])]
    all_gather x1 -> x0, waiting for transfers between devices: 58.4 us -> none  [on_device(): cache_piece = lax.all_gather(latent_cache, 'ctx', axis=1, tiled=True)]
    select_n x0 -> x2, other arithmetic: none -> 19.1 us  [doubled(): blocks = jnp.where(upper == 0, both, both[::-1]).reshape(-1, *array.shape)]
    another operation x0 -> x4, other arithmetic: none -> 15.7 us  [doubled(): both = jnp.stack([blocks, other])]
    unnamed x6 -> x13, local copies, waits for them, and re-layouts: 0.27 us -> 10.3 us
    cond x30 -> x6, local copies, waits for them, and re-layouts: 7.95 us -> 0.02 us
    ppermute x0 -> x3, starting transfers between devices: none -> 5.11 us  [doubled(): lax.ppermute(blocks, axis, [(i, i ^ distance) for i in range(length)])]
  transfers between devices with their start and end apart: 2 -> 4, of which waited for: 2 -> 4; matrix products, arithmetic and copies ran while one was open for 2% -> 0% of each run, Pallas kernels for 0% -> 0%
where the time goes in v1:
time: 323 us
  waiting for transfers between devices  189 us (59%)
  matrix products  55.1 us (17%)
  other arithmetic  46.1 us (14%)
  between operations  14.2 us (4%)
  local copies, waits for them, and re-layouts  12.2 us (4%)
  starting transfers between devices  5.11 us (2%)
    ppermute x3, waiting for transfers between devices, doubled(): lax.ppermute(blocks, axis, [(i, i ^ distance) for i in range(length)])  154 us
    reduce_scatter x1, waiting for transfers between devices, on_device(): lax.psum_scatter(lax.dot_general(w_o, head_out, (((0,), (1,)), ((), ())),...  34.8 us
    dot_general x6, matrix products, block_scores_of(): jnp.dot(query_rows, key_block, preferred_element_type=jnp.float32)  20.5 us
    select_n x2, other arithmetic, doubled(): blocks = jnp.where(upper == 0, both, both[::-1]).reshape(-1, *array.shape)  19.1 us
    dot_general x6, matrix products, latent_product(): lax.dot_general(weights.astype(jnp.bfloat16), key_block[:LATENT], (((1,),...  18.1 us
    another operation x4, other arithmetic, doubled(): both = jnp.stack([blocks, other])  15.7 us
    dot_general x1, matrix products, on_device(): lax.dot_general(w_o, head_out, (((0,), (1,)), ((), ())), preferred_elemen...  13.2 us
    unnamed x13, local copies, waits for them, and re-layouts  10.3 us
  transfers between devices with their start and end apart: 4, of which 4 were waited for; matrix products, arithmetic and copies ran while one was open for 0% of the time, Pallas kernels for 0%

profile of v1, /device:TPU:0, one launch (start us, length us, event | category | flops | bytes accessed | tf_op | source)
XLA Modules:
  0.0 322.8 jit_solution(6539666358499795412)
XLA Ops:
  6.5 0.5 collective-permute-start
  7.0 2.7 collective-permute-done
  9.7 1.5 pad_maximum_fusion.2
  11.2 3.1 fusion.20
  14.3 2.8 collective-permute-start.1
  17.2 51.9 %collective-permute-done.1 = bf16[2,576,1024]{2,1,0:T(8,128)(2,1)} collective-permute-done((bf16[2,576,1024]{2,1,0:T(8,128)(2,1)}, bf16[2,576,1024]{2,1,0:T(8,128)(2,1)}, u32[]{:S(2)}, u32[]{:S(2)}) %collective-permute-start.1) | collective-permute-done | bytes 2359328 | tf_op jit(solution)/shard_map/ppermute | solution.py:25
  69.1 2.8 pad_maximum_fusion.1
  71.9 0.0 copy-start.4
  71.9 3.6 %reverse_select_fusion.1 = bf16[2,2,576,1024]{3,2,1,0:T(8,128)(2,1)} fusion(bf16[2,2,576,1024]{3,2,1,0:T(8,128)(2,1)S(1)} %pad_maximum_fusion.1, pred[]{:T(512)S(6)} %eq.10), kind=kLoop, calls=%fused_computation.24 | loop fusion | flops 2359296 | bytes 9437185 | tf_op jit(solution)/shard_map/jit(_where)/select_n | solution.py:28
  75.5 1.8 collective-permute-start.2
  77.9 0.4 fusion.22
  78.4 0.6 copy.14
  79.0 0.2 concatenate.9
  79.2 0.1 pad_maximum_fusion.3
  79.3 99.8 %collective-permute-done.2 = bf16[4,576,1024]{2,1,0:T(8,128)(2,1)} collective-permute-done((bf16[4,576,1024]{2,1,0:T(8,128)(2,1)}, bf16[4,576,1024]{2,1,0:T(8,128)(2,1)}, u32[]{:S(2)}, u32[]{:S(2)}) %collective-permute-start.2) | collective-permute-done | bytes 4718624 | tf_op jit(solution)/shard_map/ppermute | solution.py:25
  179.1 8.3 %pad_maximum_fusion = bf16[2,4,576,1024]{3,2,1,0:T(8,128)(2,1)} fusion(bf16[1,4,576,1024]{3,2,1,0:T(8,128)(2,1)} %bitcast.10, bf16[1,4,576,1024]{3,2,1,0:T(8,128)(2,1)} %bitcast.8), kind=kLoop, calls=%fused_computation.21 | loop fusion | flops 4718592 | bytes 18874368 | tf_op jit(solution)/shard_map/stack | solution.py:26
  187.3 15.5 %reverse_select_fusion = bf16[2,4,576,1024]{3,2,1,0:T(8,128)(2,1)} fusion(bf16[2,4,576,1024]{3,2,1,0:T(8,128)(2,1)} %pad_maximum_fusion, pred[]{:T(512)S(6)} %eq.9), kind=kLoop, calls=%fused_computation.20 | loop fusion | flops 4718592 | bytes 18874368 | tf_op jit(solution)/shard_map/jit(_where)/select_n | solution.py:28
  202.8 9.0 %copy.21 = bf16[72,8,8,1024]{3,1,2,0:T(8,128)(2,1)} copy(bf16[72,8,8,1024]{3,1,0,2:T(8,128)(2,1)} %bitcast.57) | data formatting | bytes 18874368
  211.8 0.2 broadcast_in_dim.32
  212.1 49.7 %while.18 = (s32[]{:T(128)}, f32[1024]{0:T(1024)S(1)}, f32[1024]{0:T(1024)S(1)}, f32[1024,512]{1,0:T(8,128)S(1)}, s32[]{:T(128)}, /*index=5*/bf16[576,8192]{1,0:...) while((s32[]{:T(128)}, f32[1024]{0:T(1024)S(1)}, ...), condition=%wide.region_5.6_spmd.clone, body=%wide.region_0.5_spmd.clone.sunk | while | flops 2299530240 | bytes 20292124 | solution.py:114
  212.3 8.2 %conditional.3 = ((f32[1024]{0:T(1024)S(1)}, f32[1024]{0:T(1024)S(1)}, f32[1024,512]{1,0:T(8,128)S(1)})) conditional(s32[]{:T(128)} %convert_element_type.82, (f32[1024]{0:T(1024)S(1)}, f32[1024]{0:T(1024)S(1)}, f32[1024,512]{1,0:T(8,128)S(1)}) %tuple.51, (s32[]{:T(128)}, s32[64]{0:T(128)S(1)}, bf16[576,8192]{1,0:T(8,128)(2,1)}, ...), branch_computations={%region_1.1_spmd, %region_2.4_spmd} | conditional | flops 2299530240 | bytes 20291918 | solution.py:105
  212.3 0.1 broadcast_in_dim.39
  212.4 0.1 le.27
  212.4 3.4 %fusion.2 = (f32[1024]{0:T(1024)S(1)}, f32[1024,1024]{1,0:T(8,128)S(1)}) fusion(s32[1024]{0:T(1024)S(1)} %le.27, s32[1024]{0:T(1024)S(1)} %iota_add_fusion, bf16[1024,576]{1,0:T(8,128)(2,1)S(1)} %get-tuple-element.214, bf16[576,8192]{1,0:T(8,128)(2,1)} %get-tuple-element.213, s32[]{:T(128)S(6)} %select_n.36), kind=kOutput, calls=%fused_computation.3 | convolution fusion | flops 1212152832 | bytes 6565892 | tf_op jit(solution)/shard_map/while/body/eval_jaxpr/cond/branch_1_fun/dot_general | solution.py:48
  215.9 1.5 fusion.4
  217.4 3.0 multiply_add_fusion
  220.5 8.2 %conditional.3 = ((f32[1024]{0:T(1024)S(1)}, f32[1024]{0:T(1024)S(1)}, f32[1024,512]{1,0:T(8,128)S(1)})) conditional(s32[]{:T(128)} %convert_element_type.82, (f32[1024]{0:T(1024)S(1)}, f32[1024]{0:T(1024)S(1)}, f32[1024,512]{1,0:T(8,128)S(1)}) %tuple.51, (s32[]{:T(128)}, s32[64]{0:T(128)S(1)}, bf16[576,8192]{1,0:T(8,128)(2,1)}, ...), branch_computations={%region_1.1_spmd, %region_2.4_spmd} | conditional | flops 2299530240 | bytes 20291918 | solution.py:105
  220.5 0.1 broadcast_in_dim.39
  220.6 0.1 le.27
  220.7 3.4 %fusion.2 = (f32[1024]{0:T(1024)S(1)}, f32[1024,1024]{1,0:T(8,128)S(1)}) fusion(s32[1024]{0:T(1024)S(1)} %le.27, s32[1024]{0:T(1024)S(1)} %iota_add_fusion, bf16[1024,576]{1,0:T(8,128)(2,1)S(1)} %get-tuple-element.214, bf16[576,8192]{1,0:T(8,128)(2,1)} %get-tuple-element.213, s32[]{:T(128)S(6)} %select_n.36), kind=kOutput, calls=%fused_computation.3 | convolution fusion | flops 1212152832 | bytes 6565892 | tf_op jit(solution)/shard_map/while/body/eval_jaxpr/cond/branch_1_fun/dot_general | solution.py:48
  224.1 1.5 fusion.4
  225.7 3.0 multiply_add_fusion
  228.7 8.2 %conditional.3 = ((f32[1024]{0:T(1024)S(1)}, f32[1024]{0:T(1024)S(1)}, f32[1024,512]{1,0:T(8,128)S(1)})) conditional(s32[]{:T(128)} %convert_element_type.82, (f32[1024]{0:T(1024)S(1)}, f32[1024]{0:T(1024)S(1)}, f32[1024,512]{1,0:T(8,128)S(1)}) %tuple.51, (s32[]{:T(128)}, s32[64]{0:T(128)S(1)}, bf16[576,8192]{1,0:T(8,128)(2,1)}, ...), branch_computations={%region_1.1_spmd, %region_2.4_spmd} | conditional | flops 2299530240 | bytes 20291918 | solution.py:105
  228.8 0.1 broadcast_in_dim.39
  228.8 0.1 le.27
  228.9 3.4 %fusion.2 = (f32[1024]{0:T(1024)S(1)}, f32[1024,1024]{1,0:T(8,128)S(1)}) fusion(s32[1024]{0:T(1024)S(1)} %le.27, s32[1024]{0:T(1024)S(1)} %iota_add_fusion, bf16[1024,576]{1,0:T(8,128)(2,1)S(1)} %get-tuple-element.214, bf16[576,8192]{1,0:T(8,128)(2,1)} %get-tuple-element.213, s32[]{:T(128)S(6)} %select_n.36), kind=kOutput, calls=%fused_computation.3 | convolution fusion | flops 1212152832 | bytes 6565892 | tf_op jit(solution)/shard_map/while/body/eval_jaxpr/cond/branch_1_fun/dot_general | solution.py:48
  232.4 1.5 fusion.4
  233.9 3.0 multiply_add_fusion
  237.0 8.2 %conditional.3 = ((f32[1024]{0:T(1024)S(1)}, f32[1024]{0:T(1024)S(1)}, f32[1024,512]{1,0:T(8,128)S(1)})) conditional(s32[]{:T(128)} %convert_element_type.82, (f32[1024]{0:T(1024)S(1)}, f32[1024]{0:T(1024)S(1)}, f32[1024,512]{1,0:T(8,128)S(1)}) %tuple.51, (s32[]{:T(128)}, s32[64]{0:T(128)S(1)}, bf16[576,8192]{1,0:T(8,128)(2,1)}, ...), branch_computations={%region_1.1_spmd, %region_2.4_spmd} | conditional | flops 2299530240 | bytes 20291918 | solution.py:105
  237.0 0.1 broadcast_in_dim.39
  237.1 0.1 le.27
  237.2 3.4 %fusion.2 = (f32[1024]{0:T(1024)S(1)}, f32[1024,1024]{1,0:T(8,128)S(1)}) fusion(s32[1024]{0:T(1024)S(1)} %le.27, s32[1024]{0:T(1024)S(1)} %iota_add_fusion, bf16[1024,576]{1,0:T(8,128)(2,1)S(1)} %get-tuple-element.214, bf16[576,8192]{1,0:T(8,128)(2,1)} %get-tuple-element.213, s32[]{:T(128)S(6)} %select_n.36), kind=kOutput, calls=%fused_computation.3 | convolution fusion | flops 1212152832 | bytes 6565892 | tf_op jit(solution)/shard_map/while/body/eval_jaxpr/cond/branch_1_fun/dot_general | solution.py:48
  240.6 1.5 fusion.4
  242.2 3.0 multiply_add_fusion
  245.2 8.2 %conditional.3 = ((f32[1024]{0:T(1024)S(1)}, f32[1024]{0:T(1024)S(1)}, f32[1024,512]{1,0:T(8,128)S(1)})) conditional(s32[]{:T(128)} %convert_element_type.82, (f32[1024]{0:T(1024)S(1)}, f32[1024]{0:T(1024)S(1)}, f32[1024,512]{1,0:T(8,128)S(1)}) %tuple.51, (s32[]{:T(128)}, s32[64]{0:T(128)S(1)}, bf16[576,8192]{1,0:T(8,128)(2,1)}, ...), branch_computations={%region_1.1_spmd, %region_2.4_spmd} | conditional | flops 2299530240 | bytes 20291918 | solution.py:105
  245.3 0.1 broadcast_in_dim.39
  245.3 0.1 le.27
  245.4 3.4 %fusion.2 = (f32[1024]{0:T(1024)S(1)}, f32[1024,1024]{1,0:T(8,128)S(1)}) fusion(s32[1024]{0:T(1024)S(1)} %le.27, s32[1024]{0:T(1024)S(1)} %iota_add_fusion, bf16[1024,576]{1,0:T(8,128)(2,1)S(1)} %get-tuple-element.214, bf16[576,8192]{1,0:T(8,128)(2,1)} %get-tuple-element.213, s32[]{:T(128)S(6)} %select_n.36), kind=kOutput, calls=%fused_computation.3 | convolution fusion | flops 1212152832 | bytes 6565892 | tf_op jit(solution)/shard_map/while/body/eval_jaxpr/cond/branch_1_fun/dot_general | solution.py:48
  248.9 1.5 fusion.4
  250.4 3.0 multiply_add_fusion
  253.5 8.2 %conditional.3 = ((f32[1024]{0:T(1024)S(1)}, f32[1024]{0:T(1024)S(1)}, f32[1024,512]{1,0:T(8,128)S(1)})) conditional(s32[]{:T(128)} %convert_element_type.82, (f32[1024]{0:T(1024)S(1)}, f32[1024]{0:T(1024)S(1)}, f32[1024,512]{1,0:T(8,128)S(1)}) %tuple.51, (s32[]{:T(128)}, s32[64]{0:T(128)S(1)}, bf16[576,8192]{1,0:T(8,128)(2,1)}, ...), branch_computations={%region_1.1_spmd, %region_2.4_spmd} | conditional | flops 2299530240 | bytes 20291918 | solution.py:105
  253.5 0.1 broadcast_in_dim.39
  253.6 0.1 le.27
  253.7 3.4 %fusion.2 = (f32[1024]{0:T(1024)S(1)}, f32[1024,1024]{1,0:T(8,128)S(1)}) fusion(s32[1024]{0:T(1024)S(1)} %le.27, s32[1024]{0:T(1024)S(1)} %iota_add_fusion, bf16[1024,576]{1,0:T(8,128)(2,1)S(1)} %get-tuple-element.214, bf16[576,8192]{1,0:T(8,128)(2,1)} %get-tuple-element.213, s32[]{:T(128)S(6)} %select_n.36), kind=kOutput, calls=%fused_computation.3 | convolution fusion | flops 1212152832 | bytes 6565892 | tf_op jit(solution)/shard_map/while/body/eval_jaxpr/cond/branch_1_fun/dot_general | solution.py:48
  257.1 1.5 fusion.4
  258.7 3.0 multiply_add_fusion
  261.8 1.3 copy-done.2
  263.1 1.9 broadcast_divide_fusion
  265.0 1.4 fusion.21
  266.4 1.5 fusion.24
  267.9 0.0 copy-start.1
  267.9 13.2 %fusion.18 = bf16[7168,64]{0,1:T(8,128)(2,1)} fusion(bf16[2048,7168]{1,0:T(8,128)(2,1)} %param.15, bf16[16,8,8,128]{3,2,1,0:T(8,128)(2,1)S(1)} %fusion.24), kind=kOutput, calls=%fused_computation.23 | convolution fusion | flops 1879506944 | bytes 30539776 | tf_op jit(solution)/shard_map/dot_general | solution.py:119
  281.1 0.0 reduce-scatter.2.cloned.1.call-update
  281.2 34.8 %reduce-scatter.2.cloned.1.call-done = bf16[1792,64]{0,1:T(8,128)(2,1)} async-done(((bf16[7168,64]{0,1:T(8,128)(2,1)}), bf16[1792,64]{0,1:T(8,128)(2,1)}) %reduce-scatter.2.cloned.1.call-update) | async-done | bytes 229392 | tf_op jit(solution)/shard_map/reduce_scatter | solution.py:118
  (39 shorter events, 0.2 us)
Async XLA Ops:
  6.5 71.4 %copy-start = (bf16[16,128,512]{2,1,0:T(8,128)(2,1)S(1)}, bf16[16,128,512]{2,1,0:T(8,128)(2,1)}, u32[]{:S(2)}) copy-start(bf16[16,128,512]{2,1,0:T(8,128)(2,1)} %param.13) | copy-start | bytes 6291460
  6.5 309.4 %reduce-scatter.2.cloned.1.call-start = ((), (), s32[]{:S(2)}) async-start(), calls=%async_computation.1 | async-start | bytes 1146880 | tf_op jit(solution)/shard_map/reduce_scatter | solution.py:118
  6.5 3.2 collective-permute-start
  14.3 54.7 %collective-permute-start.1 = (bf16[2,576,1024]{2,1,0:T(8,128)(2,1)}, bf16[2,576,1024]{2,1,0:T(8,128)(2,1)}, u32[]{:S(2)}, u32[]{:S(2)}) collective-permute-start(bf16[2,576,1024]{2,1,0:T(8,128)(2,1)} %get-tuple-element.277), channel_id=1, source_target_pairs={{0,8},{4,12},{8,0},{12,4},{16,24},{20,28},{24,16},{28,20},{1,9},{5... | collective-permute-start | bytes 7077896 | tf_op jit(solution)/shard_map/ppermute | solution.py:25
  71.9 6.0 %copy-start.4 = (bf16[64,2048]{1,0:T(8,128)(2,1)S(1)}, bf16[64,2048]{1,0:T(8,128)(2,1)}, u32[]{:S(2)}) copy-start(bf16[64,2048]{1,0:T(8,128)(2,1)} %param.11) | copy-start | bytes 786436
  75.5 103.6 %collective-permute-start.2 = (bf16[4,576,1024]{2,1,0:T(8,128)(2,1)}, bf16[4,576,1024]{2,1,0:T(8,128)(2,1)}, u32[]{:S(2)}, u32[]{:S(2)}) collective-permute-start(bf16[4,576,1024]{2,1,0:T(8,128)(2,1)} %bitcast.9), channel_id=1, source_target_pairs={{0,16},{4,20},{8,24},{12,28},{16,0},{20,4},{24,8},{28,12},{1,17},{... | collective-permute-start | bytes 14155784 | tf_op jit(solution)/shard_map/ppermute | solution.py:25
  77.9 1.0 copy-start.5
  261.8 1.3 copy-start.2
  261.8 3.2 copy-start.3
  267.9 48.1 %copy-start.1 = (bf16[16,128,512]{2,1,0:T(8,128)(2,1)S(1)}, bf16[16,128,512]{2,1,0:T(8,128)(2,1)}, u32[]{:S(2)}) copy-start(bf16[16,128,512]{2,1,0:T(8,128)(2,1)} %param.13) | copy-start | bytes 6291460
Sparse Core Ops, SparseCore 0:
  281.3 34.6 reduce-scatter.1
